TPU v7x, 32 devices: a whole 2x2x4 slice. The times are simulated.
32 devices in a mesh: dp: 4 (over x, core), expert: 8 (over z, y).
Axes of the slice: x: 2, y: 2, z: 4, core: 2. Of those that a mesh axis runs over, the one named last changes fastest.
Arguments:
- tokens: bfloat16 [16384, 768], P(('dp', 'expert')), may hold values from -6 to 6
- cotangent: bfloat16 [16384, 768], P(('dp', 'expert')), may hold values from -6 to 6
- chosen: int32 [16384, 2], P(('dp', 'expert')), may hold values from 0 to 9, all different within a row; in each aligned block of 512 rows (0 to 511, 512 to 1023, ...) at most 128 rows name the same one
- gates: float32 [16384, 2], P(('dp', 'expert')), may hold values from 0.2 to 0.8
- lengths: int32 [32, 8], P(('dp', 'expert')), may hold values from 1 to 256, 512 in all within a row
- keep_mask: int32 [16384], P(('dp', 'expert')), may hold values 0 or 1
- gain1: float32 [768], replicated, may hold values from 0.5 to 1.5
- w_qkv: bfloat16 [768, 2304], replicated, may hold values from -0.21875 to 0.21875
- w_o: bfloat16 [768, 768], replicated, may hold values from -0.875 to 0.875
- gain2: float32 [768], replicated, may hold values from 0.5 to 1.5
- frozen_in: bfloat16 [2, 3072, 768], replicated, may hold values from -0.21875 to 0.21875
- frozen_out: bfloat16 [2, 3072, 768], replicated, may hold values from -0.109375 to 0.109375
- w_in: bfloat16 [8, 3072, 768], P('expert', 'dp'), may hold values from -0.21875 to 0.21875
- w_out: bfloat16 [8, 3072, 768], P('expert', 'dp'), may hold values from -0.109375 to 0.109375
Outputs:
- output: bfloat16 [16384, 768], P(('dp', 'expert'))
- d_tokens: bfloat16 [16384, 768], P(('dp', 'expert'))
- d_gain1: float32 [768], replicated
- d_w_qkv: float32 [768, 2304], replicated
- d_w_o: float32 [768, 768], replicated
- d_gain2: float32 [768], replicated
- d_w_in: float32 [8, 3072, 768], P('expert', 'dp')
- d_w_out: float32 [8, 3072, 768], P('expert', 'dp')
- counts: float32 [10], replicated
Inputs may be any that keep to these rules, and one draw needn't show every extreme that they name: `chosen`: each token names two different experts; among the 512 tokens of one device no expert is named more than 128 times, a bound that some block reaches. The 8 lengths of a device sum to 512; the longest is exactly 256.
All inputs are finite; a program needn't handle non-finite values. No bound on the sum of `keep_mask` on one device may be relied on, other than what follows from the above.
Results may differ from a plain program's by a relative error of at most 0.012.
Values may be sent and summed in bfloat16 or wider, within the bound.
A program may use at most 256 MiB of HBM per device.

v0:
```python
import jax
import jax.numpy as jnp
from jax import lax
from jax.sharding import PartitionSpec as P

HEADS = 12
HEAD_DIM = 64
FROZEN = 2


def layer_norm(values_in, gain_vec):
    row_mean = jnp.mean(values_in, axis=-1, keepdims=True)
    centred = values_in - row_mean
    variance = jnp.mean(centred * centred, axis=-1, keepdims=True)
    return centred * lax.rsqrt(variance + 1e-05) * gain_vec


def expert_forward(rows_low, up_weights, down_weights):
    hidden = jnp.einsum("gcd,gfd->gcf", rows_low, up_weights, preferred_element_type=jnp.float32)
    active = jax.nn.gelu(hidden).astype(jnp.bfloat16)
    result_rows = jnp.einsum(
        "gcf,gfd->gcd", active, down_weights, preferred_element_type=jnp.float32
    ).astype(jnp.bfloat16)
    return (result_rows, hidden)


def expert_backward(result_grad, hidden, up_weights, down_weights):
    active_grad = jnp.einsum(
        "gcd,gfd->gcf", result_grad, down_weights, preferred_element_type=jnp.float32
    )
    active, gelu_back = jax.vjp(jax.nn.gelu, hidden)
    hidden_grad = gelu_back(active_grad)[0].astype(jnp.bfloat16)
    input_grad = jnp.einsum(
        "gcf,gfd->gcd", hidden_grad, up_weights, preferred_element_type=jnp.float32
    ).astype(jnp.bfloat16)
    return (input_grad, hidden_grad, active.astype(jnp.bfloat16))


def block_scores(query_part, key_heads, allowed):
    scores = (
        jnp.einsum("qhd,khd->hqk", query_part, key_heads, preferred_element_type=jnp.float32)
        * 0.125
    )
    return jnp.where(allowed[None], scores, -1e30)


def body(
    tokens,
    cotangent,
    chosen,
    gates,
    lengths,
    keep_mask,
    gain1,
    w_qkv,
    w_o,
    gain2,
    frozen_in,
    frozen_out,
    w_in,
    w_out,
):
    row_count = tokens.shape[0]
    feat_width = tokens.shape[1]
    owners = lax.axis_size("expert")
    kind_count = FROZEN + owners
    slot_count = (2 * row_count * 5 // (4 * kind_count) + 7) // 8 * 8
    block_rows = min(512, row_count)
    weights_in, weights_out = (
        lax.all_gather(w_in, "dp", axis=1, tiled=True),
        lax.all_gather(w_out, "dp", axis=1, tiled=True),
    )
    tokens_full = tokens.astype(jnp.float32)
    normed_one, norm_one_back = jax.vjp(layer_norm, tokens_full, gain1)
    normed_one_low = normed_one.astype(jnp.bfloat16)
    projected = jnp.dot(normed_one_low, w_qkv, preferred_element_type=jnp.float32).astype(
        jnp.bfloat16
    )
    queries = projected[:, :feat_width].reshape(row_count, HEADS, HEAD_DIM)
    key_heads = projected[:, feat_width : 2 * feat_width].reshape(row_count, HEADS, HEAD_DIM)
    value_heads = projected[:, 2 * feat_width :].reshape(row_count, HEADS, HEAD_DIM)
    places = jnp.arange(row_count, dtype=jnp.int32)
    doc_ends = jnp.cumsum(lengths[0])
    documents = jnp.sum((places[:, None] >= doc_ends[None, :]).astype(jnp.int32), axis=1)

    def permitted():
        return (
            (documents[:, None] == documents[None, :])
            & (places[None, :] <= places[:, None])
            & ((keep_mask[None, :] > 0) | (places[None, :] == places[:, None]))
        )

    scores = block_scores(queries, key_heads, permitted())
    peak_score = jnp.max(scores, axis=-1, keepdims=True)
    exp_scores = jnp.exp(scores - peak_score)
    exp_total = jnp.sum(exp_scores, axis=-1, keepdims=True)
    probs_low = (exp_scores / exp_total).astype(jnp.bfloat16)
    block_out = jnp.einsum(
        "hqk,khd->qhd", probs_low, value_heads, preferred_element_type=jnp.float32
    )
    out_blocks = block_out.reshape(block_rows, feat_width).astype(jnp.bfloat16)
    lse_blocks = [peak_score + jnp.log(exp_total)]
    mixed_rows = tokens_full + jnp.dot(out_blocks, w_o, preferred_element_type=jnp.float32)
    normed_two, norm_two_back = jax.vjp(layer_norm, mixed_rows, gain2)
    normed_two_low = normed_two.astype(jnp.bfloat16)
    flat_ids = chosen.reshape(-1)
    one_hot = (flat_ids[:, None] == jnp.arange(kind_count, dtype=jnp.int32)[None, :]).astype(
        jnp.int32
    )
    slot_ranks = jnp.sum(jnp.cumsum(one_hot, axis=0) * one_hot, axis=1) - 1
    positions = flat_ids * slot_count + slot_ranks
    buffer_rows = (
        jnp.zeros((kind_count * slot_count, feat_width), jnp.bfloat16)
        .at[positions]
        .set(jnp.repeat(normed_two_low, 2, axis=0))
    )
    local_rows = buffer_rows[: FROZEN * slot_count].reshape(FROZEN, slot_count, feat_width)
    routed_rows = buffer_rows[FROZEN * slot_count :].reshape(owners, slot_count, feat_width)
    arrived_rows = lax.all_to_all(routed_rows, "expert", split_axis=0, concat_axis=0, tiled=True)
    result_rows, _ = expert_forward(
        arrived_rows.reshape(1, -1, feat_width), weights_in, weights_out
    )
    served = result_rows.reshape(arrived_rows.shape)
    frozen_result, frozen_hidden = expert_forward(local_rows, frozen_in, frozen_out)
    returned = lax.all_to_all(served, "expert", split_axis=0, concat_axis=0, tiled=True)
    results = jnp.concatenate(
        [frozen_result.reshape(-1, feat_width), returned.reshape(-1, feat_width)], axis=0
    )
    picked = results[positions].astype(jnp.float32).reshape(row_count, 2, feat_width)
    output = mixed_rows + jnp.sum(picked * gates[:, :, None], axis=1)
    grad_out = cotangent.astype(jnp.float32)
    weighted = (jnp.repeat(grad_out, 2, axis=0) * gates.reshape(-1, 1)).astype(jnp.bfloat16)
    grad_buffer = (
        jnp.zeros((kind_count * slot_count, feat_width), jnp.bfloat16).at[positions].set(weighted)
    )
    frozen_grad_rows = grad_buffer[: FROZEN * slot_count].reshape(FROZEN, slot_count, feat_width)
    routed_grad = grad_buffer[FROZEN * slot_count :].reshape(owners, slot_count, feat_width)
    arrived_grad = lax.all_to_all(routed_grad, "expert", split_axis=0, concat_axis=0, tiled=True)
    flat_rows = arrived_rows.reshape(1, -1, feat_width)
    flat_grad = arrived_grad.reshape(1, -1, feat_width)
    hidden_all = jnp.einsum(
        "gcd,gfd->gcf", flat_rows, weights_in, preferred_element_type=jnp.float32
    )
    row_input_grad, hidden_grad, active = expert_backward(
        flat_grad, hidden_all, weights_in, weights_out
    )
    sent_back = lax.all_to_all(
        row_input_grad.reshape(owners, slot_count, feat_width),
        "expert",
        split_axis=0,
        concat_axis=0,
        tiled=True,
    )
    frozen_input_grad, _, _ = expert_backward(
        frozen_grad_rows, frozen_hidden, frozen_in, frozen_out
    )
    hidden_rows = hidden_grad[0]
    active_rows = active[0]
    input_rows = flat_rows[0]
    output_rows = flat_grad[0]
    term_in = lax.dot_general(
        hidden_rows, input_rows, (((0,), (0,)), ((), ())), preferred_element_type=jnp.float32
    )
    term_out = lax.dot_general(
        active_rows, output_rows, (((0,), (0,)), ((), ())), preferred_element_type=jnp.float32
    )
    summed = lax.psum_scatter(
        jnp.concatenate([term_in, term_out], axis=1), "dp", scatter_dimension=0, tiled=True
    )
    d_w_in = summed[:, :feat_width][None]
    d_w_out = summed[:, feat_width:][None]
    row_grads = jnp.concatenate(
        [frozen_input_grad.reshape(-1, feat_width), sent_back.reshape(-1, feat_width)], axis=0
    )
    normed_two_grad = jnp.sum(
        row_grads[positions].astype(jnp.float32).reshape(row_count, 2, feat_width), axis=1
    )
    mixed_part, gain2_grad = norm_two_back(normed_two_grad)
    mixed_grad = grad_out + mixed_part
    branch_grad = mixed_grad.astype(jnp.bfloat16)
    w_o_grad = lax.dot_general(
        out_blocks, branch_grad, (((0,), (0,)), ((), ())), preferred_element_type=jnp.float32
    )
    attended_grad = lax.dot_general(
        branch_grad, w_o, (((1,), (1,)), ((), ())), preferred_element_type=jnp.float32
    ).astype(jnp.bfloat16)
    attended_heads = attended_grad.reshape(row_count, HEADS, HEAD_DIM)
    key_grad = jnp.zeros((row_count, HEADS, HEAD_DIM), jnp.float32)
    value_grad = jnp.zeros((row_count, HEADS, HEAD_DIM), jnp.float32)
    query_grads = []
    for block_index, row_start in enumerate(range(0, row_count, block_rows)):
        scores = block_scores(queries, key_heads, permitted())
        probs_full = jnp.exp(scores - lse_blocks[block_index])
        probs_low = probs_full.astype(jnp.bfloat16)
        prob_grad = jnp.einsum(
            "qhd,khd->hqk", attended_heads, value_heads, preferred_element_type=jnp.float32
        )
        row_delta = jnp.sum(probs_full * prob_grad, axis=-1, keepdims=True)
        score_grad = (probs_full * (prob_grad - row_delta)).astype(jnp.bfloat16)
        query_grads.append(
            jnp.einsum("hqk,khd->qhd", score_grad, key_heads, preferred_element_type=jnp.float32)
            * 0.125
        )
        key_grad = (
            jnp.einsum("hqk,qhd->khd", score_grad, queries, preferred_element_type=jnp.float32)
            * 0.125
        )
        value_grad = jnp.einsum(
            "hqk,qhd->khd", probs_low, attended_heads, preferred_element_type=jnp.float32
        )
    projected_grad = jnp.concatenate(
        [
            query_grads[0].reshape(row_count, feat_width),
            key_grad.reshape(row_count, feat_width),
            value_grad.reshape(row_count, feat_width),
        ],
        axis=1,
    ).astype(jnp.bfloat16)
    w_qkv_grad = lax.dot_general(
        normed_one_low, projected_grad, (((0,), (0,)), ((), ())), preferred_element_type=jnp.float32
    )
    normed_one_grad = lax.dot_general(
        projected_grad, w_qkv, (((1,), (1,)), ((), ())), preferred_element_type=jnp.float32
    )
    tokens_part, gain1_grad = norm_one_back(normed_one_grad)
    tokens_grad = (mixed_grad + tokens_part).astype(jnp.bfloat16)
    local_counts = jnp.sum(one_hot, axis=0).astype(jnp.float32)
    gain1_sum, w_qkv_sum, w_o_sum, gain2_sum, counts = lax.psum(
        (gain1_grad, w_qkv_grad, w_o_grad, gain2_grad, local_counts), ("dp", "expert")
    )
    return (
        output.astype(jnp.bfloat16),
        tokens_grad,
        gain1_sum,
        w_qkv_sum,
        w_o_sum,
        gain2_sum,
        d_w_in,
        d_w_out,
        counts,
    )


def solution(mesh):
    placed = (
        P(("dp", "expert"), None),
        P(("dp", "expert"), None),
        P(("dp", "expert"), None),
        P(("dp", "expert"), None),
        P(("dp", "expert"), None),
        P(("dp", "expert")),
        P(),
        P(),
        P(),
        P(),
        P(),
        P(),
        P("expert", "dp", None),
        P("expert", "dp", None),
    )
    return jax.shard_map(
        body,
        mesh=mesh,
        in_specs=placed,
        out_specs=(
            P(("dp", "expert"), None),
            P(("dp", "expert"), None),
            P(),
            P(),
            P(),
            P(),
            P("expert", "dp", None),
            P("expert", "dp", None),
            P(),
        ),
        check_vma=False,
    )
```

profile of v0, /device:TPU:0, one launch (start us, length us, event | category | flops | bytes accessed | tf_op | source)
XLA Modules:
  0.0 601.5 jit_solution(12574793378495375460)
XLA Ops:
  71.9 7.2 %scatter_custom_fusion = bf16[1280,768]{1,0:T(8,128)(2,1)} fusion(s32[1024]{0:T(1024)S(1)} %bitcast.116, bf16[1024,768]{1,0:T(8,128)(2,1)} %reshape.407, bf16[]{:T(256)} %constant.25.clone.1), kind=kCustom, calls=%fused_computation.98 | custom fusion | bytes 1966592 | tf_op jit(solution)/shard_map/scatter | solution.py:115
  81.8 7.3 %all-to-all-start = ((bf16[8,128,768]{2,1,0:T(8,128)(2,1)}), bf16[8,128,768]{2,1,0:T(8,128)(2,1)}, u32[]{:S(2)}, u32[]{:S(2)}) async-start(bf16[8,128,768]{2,1,0:T(8,128)(2,1)} %bitcast.96), calls=%async_computation | async-start | bytes 3145728 | tf_op jit(solution)/shard_map/all_to_all | solution.py:119
  100.8 8.1 %scatter_custom_fusion.1 = bf16[1280,768]{1,0:T(8,128)(2,1)} fusion(s32[1024]{0:T(1024)S(1)} %bitcast.117, f32[1024,768]{1,0:T(8,128)} %reshape.374, f32[1024]{0:T(1024)S(1)} %mul.298, bf16[]{:T(256)} %constant.25.clone.1), kind=kCustom, calls=%fused_computation.71 | custom fusion | flops 1572864 | bytes 5115906 | tf_op jit(solution)/shard_map/scatter | solution.py:134
  111.5 14.8 %all-to-all-done = bf16[8,128,768]{2,1,0:T(8,128)(2,1)} async-done(((bf16[8,128,768]{2,1,0:T(8,128)(2,1)}), bf16[8,128,768]{2,1,0:T(8,128)(2,1)}, u32[]{:S(2)}, u32[]{:S(2)}) %all-to-all-start) | async-done | bytes 1572896 | tf_op jit(solution)/shard_map/all_to_all | solution.py:119
  130.6 10.3 %fusion.19 = f32[1024,3072]{1,0:T(8,128)} fusion(bf16[1024,768]{1,0:T(8,128)(2,1)} %bitcast.14, bf16[1,3072,768]{2,1,0:T(8,128)(2,1)} %all-gather.3.cloned.1.call-done), kind=kOutput, calls=%fused_computation.32 | convolution fusion | flops 4831838208 | bytes 18874368 | tf_op jit(solution)/shard_map/gcd,gfd->gcf/dot_general | solution.py:19
  140.9 26.3 %all-to-all-done.2 = bf16[8,128,768]{2,1,0:T(8,128)(2,1)} async-done(((bf16[8,128,768]{2,1,0:T(8,128)(2,1)}), bf16[8,128,768]{2,1,0:T(8,128)(2,1)}, u32[]{:S(2)}, u32[]{:S(2)}) %all-to-all-start.2) | async-done | bytes 1572896 | tf_op jit(solution)/shard_map/all_to_all | solution.py:138
  167.2 11.3 %fusion.98 = f32[3072,768]{0,1:T(8,128)} fusion(bf16[1024,768]{1,0:T(8,128)(2,1)} %bitcast.22, f32[1024,3072]{1,0:T(8,128)} %fusion.19), kind=kOutput, calls=%fused_computation.147 | convolution fusion | flops 4860149760 | bytes 23592960 | tf_op jit(solution)/shard_map/dot_general | solution.py:164
  178.5 15.7 %fusion.6 = bf16[1024,3072]{1,0:T(8,128)(2,1)S(1)} fusion(f32[1024,3072]{1,0:T(8,128)} %fusion.19, bf16[1024,768]{1,0:T(8,128)(2,1)} %bitcast.22, bf16[1,3072,768]{2,1,0:T(8,128)(2,1)} %all-gather.5.cloned.1.call-done), kind=kOutput, calls=%fused_computation.13 | convolution fusion | flops 4894752768 | bytes 25165824 | tf_op jit(solution)/shard_map/gcd,gfd->gcf/dot_general | solution.py:28
  194.3 8.3 %fusion.105 = f32[3072,768]{0,1:T(8,128)S(1)} fusion(bf16[1024,3072]{1,0:T(8,128)(2,1)S(1)} %fusion.6, bf16[1024,768]{1,0:T(8,128)(2,1)} %bitcast.14), kind=kOutput, calls=%fused_computation.153 | convolution fusion | flops 4831838208 | bytes 17301504 | tf_op jit(solution)/shard_map/dot_general | solution.py:161
  202.6 6.9 %pad_maximum_fusion = f32[3072,1536]{0,1:T(8,128)} fusion(f32[3072,768]{0,1:T(8,128)S(1)} %copy-done.11, f32[3072,768]{0,1:T(8,128)S(1)} %fusion.105), kind=kLoop, calls=%fused_computation.4 | loop fusion | flops 4718592 | bytes 37748736 | tf_op jit(solution)/shard_map/concatenate | solution.py:168
  209.5 12.5 %fusion.40 = bf16[1024,768]{1,0:T(8,128)(2,1)} fusion(bf16[1,3072,768]{2,1,0:T(8,128)(2,1)} %all-gather.5.cloned.1.call-done, f32[1024,3072]{1,0:T(8,128)} %fusion.19), kind=kOutput, calls=%fused_computation.65 | convolution fusion | flops 4860936192 | bytes 18874368 | tf_op jit(solution)/shard_map/gcf,gfd->gcd/dot_general | solution.py:21
  229.5 8.9 %fusion.104 = f32[2,128,3072]{2,1,0:T(8,128)S(1)} fusion(bf16[2,128,768]{2,1,0:T(8,128)(2,1)S(1)} %bitcast.104, bf16[2,3072,768]{2,1,0:T(8,128)(2,1)} %param.24), kind=kOutput, calls=%fused_computation.152 | convolution fusion | flops 1207959552 | bytes 12976128 | tf_op jit(solution)/shard_map/gcd,gfd->gcf/dot_general | solution.py:19
  238.4 7.5 %fusion.63 = bf16[2,128,768]{2,1,0:T(8,128)(2,1)} fusion(bf16[2,3072,768]{2,1,0:T(8,128)(2,1)} %param.25, f32[2,128,3072]{2,1,0:T(8,128)S(1)} %fusion.104), kind=kOutput, calls=%fused_computation.91 | convolution fusion | flops 1215234048 | bytes 12976128 | tf_op jit(solution)/shard_map/gcf,gfd->gcd/dot_general | solution.py:21
  252.1 11.0 %all-to-all-done.1 = bf16[8,128,768]{2,1,0:T(8,128)(2,1)} async-done(((bf16[8,128,768]{2,1,0:T(8,128)(2,1)}), bf16[8,128,768]{2,1,0:T(8,128)(2,1)}, u32[]{:S(2)}, u32[]{:S(2)}) %all-to-all-start.1) | async-done | bytes 1572896 | tf_op jit(solution)/shard_map/all_to_all | solution.py:125
  268.9 13.3 %fusion.60 = bf16[2,128,768]{2,1,0:T(8,128)(2,1)} fusion(bf16[2,3072,768]{2,1,0:T(8,128)(2,1)} %param.24, f32[2,128,3072]{2,1,0:T(8,128)} %copy-done.19, bf16[2,128,768]{2,1,0:T(8,128)(2,1)} %bitcast.111, bf16[2,3072,768]{2,1,0:T(8,128)(2,1)} %param.25), kind=kOutput, calls=%fused_computation.90 | convolution fusion | flops 2431844352 | bytes 22806528 | tf_op jit(solution)/shard_map/gcf,gfd->gcd/dot_general | solution.py:33
  285.1 7.6 %gather_fusion = bf16[1024,768]{1,0:T(8,128)(2,1)} fusion(bf16[1280,768]{1,0:T(8,128)(2,1)} %pad_maximum_fusion.2, s32[1024]{0:T(1024)S(1)} %broadcast_clamp_fusion), kind=kCustom, calls=%fused_computation | custom fusion | bytes 3149824 | tf_op jit(solution)/shard_map/gather | solution.py:129
  292.7 11.4 %all-to-all-done.3 = bf16[8,128,768]{2,1,0:T(8,128)(2,1)} async-done(((bf16[8,128,768]{2,1,0:T(8,128)(2,1)}), bf16[8,128,768]{2,1,0:T(8,128)(2,1)}, u32[]{:S(2)}, u32[]{:S(2)}) %all-to-all-start.3) | async-done | bytes 1572896 | tf_op jit(solution)/shard_map/all_to_all | solution.py:147
  307.0 7.4 %gather_fusion.1 = bf16[1024,768]{1,0:T(8,128)(2,1)} fusion(bf16[1280,768]{1,0:T(8,128)(2,1)} %pad_maximum_fusion.3, s32[1024]{0:T(1024)S(1)} %broadcast_clamp_fusion), kind=kCustom, calls=%fused_computation.1 | custom fusion | bytes 3149824 | tf_op jit(solution)/shard_map/gather | solution.py:176
  324.2 6.8 %reduce_sum.185 = f32[512,768]{1,0:T(8,128)} reduce(f32[512,2,768]{2,1,0:T(2,128)} %reshape.386, f32[]{:T(128)} %constant.18.clone.1), dimensions={1}, to_apply=%region_14.15 | reduce | flops 393216 | bytes 4718596 | tf_op jit(solution)/shard_map/reduce_sum | solution.py:175
  334.2 16.6 %multiply_reduce_fusion.1 = f32[512,768]{1,0:T(8,128)S(1)} fusion(f32[512,2,768]{2,1,0:T(2,128)S(1)} %copy-done.6, f32[512,2]{1,0:T(8,128)} %copy.66), kind=kLoop, calls=%fused_computation.46 | loop fusion | flops 1179648 | bytes 4722688 | tf_op jit(solution)/shard_map/reduce_sum | solution.py:130
  362.0 11.0 %multiply_reduce_fusion = (f32[12,512]{1,0:T(8,128)S(1)}, f32[12,512,512]{1,2,0:T(8,128)}) fusion(f32[12,512]{1,0:T(8,128)S(1)} %copy-done.25, f32[12,512,512]{1,2,0:T(8,128)} %copy-done.1, pred[512,512]{0,1:T(8,128)(4,1)S(1)} %copy-done.15, bf16[512,12,64]{0,2,1:T(8,128)(2,1)S(1)} %bitcast.100, bf16[512,12,64]{0,2,1:T(8,128)(2,1)S(1)} %bitcast.99), kind=kOutput, calls=%fused_computation.15 | convolution fusion | flops 418375680 | bytes 27049984 | tf_op jit(solution)/shard_map/qhd,khd->hqk/dot_general | solution.py:195
  374.5 7.0 %multiply_convert_fusion = bf16[12,512,512]{1,2,0:T(8,128)(2,1)S(1)} fusion(f32[12,512,512]{1,2,0:T(8,128)} %get-tuple-element.60, f32[12,512]{1,0:T(8,128)S(1)} %get-tuple-element.59, f32[12,512]{1,0:T(8,128)S(1)} %copy-done.25, f32[12,512,512]{1,2,0:T(8,128)S(1)} %bitcast.91, pred[512,512]{0,1:T(8,128)(4,1)S(1)} %copy-done.15), kind=kLoop, calls=%fused_computation.14 | loop fusion | flops 18874368 | bytes 31768576 | tf_op jit(solution)/shard_map/convert_element_type | solution.py:199
  402.1 40.2 %all-reduce = (f32[768]{0:T(1024)}, f32[768]{0:T(1024)}, f32[10]{0:T(128)}) all-reduce(f32[768]{0:T(1024)} %get-tuple-element.38, f32[768]{0:T(1024)} %get-tuple-element.36, f32[10]{0:T(128)} %convert_element_type.136), channel_id=1, replica_groups=mesh['dp'=4,'expert'=8] {'dp','expert'}, use_global_device_ids=true, to_apply=%region_21.22 | all-reduce | flops 1546 | bytes 12368 | tf_op jit(solution)/shard_map/psum | solution.py:228
  458.0 128.8 %all-reduce.4.cloned.1.call-done = (f32[768,2304]{1,0:T(8,128)}, f32[768,768]{1,0:T(8,128)}) async-done(((f32[768,2304]{1,0:T(8,128)}, f32[768,768]{1,0:T(8,128)}), (f32[768,2304]{1,0:T(8,128)}, f32[768,768]{1,0:T(8,128)})) %all-reduce.4.cloned.1.call-update) | async-done | bytes 9437200 | tf_op jit(solution)/shard_map/psum | solution.py:228
  (210 shorter events, 180.6 us)
Async XLA Ops:
  7.2 20.0 %copy-start = (bf16[768,2304]{1,0:T(8,128)(2,1)S(1)}, bf16[768,2304]{1,0:T(8,128)(2,1)}, u32[]{:S(2)}) copy-start(bf16[768,2304]{1,0:T(8,128)(2,1)} %param.21) | copy-start | bytes 10616836
  7.2 123.4 %all-gather.3.cloned.1.call-start = ((), (), s32[]{:S(2)}) async-start(), calls=%async_computation.5 | async-start | bytes 5898240 | tf_op jit(solution)/shard_map/all_gather | solution.py:70
  9.6 22.3 %copy-start.31 = (f32[512]{0:T(512)}, f32[512]{0:T(512)S(1)}, u32[]{:S(2)}) copy-start(f32[512]{0:T(512)S(1)} %broadcast_multiply_fusion.2) | copy-start | bytes 6148
  11.1 12.5 %copy-start.37 = (f32[512]{0:T(512)}, f32[512]{0:T(512)S(1)}, u32[]{:S(2)}) copy-start(f32[512]{0:T(512)S(1)} %fusion.45) | copy-start | bytes 6148
  11.1 20.7 %copy-start.35 = (f32[512]{0:T(512)}, f32[512]{0:T(512)S(1)}, u32[]{:S(2)}) copy-start(f32[512]{0:T(512)S(1)} %fusion.77) | copy-start | bytes 6148
  79.1 10.7 %copy-start.44 = (f32[512,2]{0,1:T(2,128)S(1)}, f32[512,2]{0,1:T(2,128)}, u32[]{:S(2)}) copy-start(f32[512,2]{0,1:T(2,128)} %param.17) | copy-start | bytes 12292
  81.8 44.5 %all-to-all-start = ((bf16[8,128,768]{2,1,0:T(8,128)(2,1)}), bf16[8,128,768]{2,1,0:T(8,128)(2,1)}, u32[]{:S(2)}, u32[]{:S(2)}) async-start(bf16[8,128,768]{2,1,0:T(8,128)(2,1)} %bitcast.96), calls=%async_computation | async-start | bytes 3145728 | tf_op jit(solution)/shard_map/all_to_all | solution.py:119
  89.1 89.4 %all-gather.5.cloned.1.call-start = ((), (), s32[]{:S(2)}) async-start(), calls=%async_computation.6 | async-start | bytes 5898240 | tf_op jit(solution)/shard_map/all_gather | solution.py:71
  126.2 40.9 %all-to-all-start.2 = ((bf16[8,128,768]{2,1,0:T(8,128)(2,1)}), bf16[8,128,768]{2,1,0:T(8,128)(2,1)}, u32[]{:S(2)}, u32[]{:S(2)}) async-start(bf16[8,128,768]{2,1,0:T(8,128)(2,1)} %bitcast.97), calls=%async_computation.2 | async-start | bytes 3145728 | tf_op jit(solution)/shard_map/all_to_all | solution.py:138
  130.5 316.4 %reduce-scatter.2.cloned.1.call-start = ((), (), s32[]{:S(2)}) async-start(), calls=%async_computation.7 | async-start | bytes 23592960 | tf_op jit(solution)/shard_map/reduce_scatter | solution.py:167
  194.3 8.3 %copy-start.49 = (bf16[1024,3072]{1,0:T(8,128)(2,1)}, bf16[1024,3072]{1,0:T(8,128)(2,1)S(1)}, u32[]{:S(2)}) copy-start(bf16[1024,3072]{1,0:T(8,128)(2,1)S(1)} %fusion.6) | copy-start | bytes 18874372
  194.3 8.3 %copy-start.11 = (f32[3072,768]{0,1:T(8,128)S(1)}, f32[3072,768]{0,1:T(8,128)}, u32[]{:S(2)}) copy-start(f32[3072,768]{0,1:T(8,128)} %fusion.98) | copy-start | bytes 28311556
  222.0 41.1 %all-to-all-start.1 = ((bf16[8,128,768]{2,1,0:T(8,128)(2,1)}), bf16[8,128,768]{2,1,0:T(8,128)(2,1)}, u32[]{:S(2)}, u32[]{:S(2)}) async-start(bf16[8,128,768]{2,1,0:T(8,128)(2,1)} %bitcast.106), calls=%async_computation.1 | async-start | bytes 3145728 | tf_op jit(solution)/shard_map/all_to_all | solution.py:125
  229.5 16.4 %slice-start.3 = ((s8[4718592]{0:T(1024)(128)(4,1)}), s8[524288]{0:T(1024)(128)(4,1)S(1)}, s32[]{:S(2)}) async-start(s8[4718592]{0:T(1024)(128)(4,1)} %bitcast.122), calls=%async_computation.12 | async-start | bytes 1048576
  229.5 16.4 %slice-start.5 = ((s8[6291456]{0:T(1024)(128)(4,1)}), s8[4194304]{0:T(1024)(128)(4,1)S(1)}, s32[]{:S(2)}) async-start(s8[6291456]{0:T(1024)(128)(4,1)} %bitcast.127), calls=%async_computation.14 | async-start | bytes 8388608
  238.4 7.5 %slice-start.4 = ((s8[4718592]{0:T(1024)(128)(4,1)}), s8[4194304]{0:T(1024)(128)(4,1)S(1)}, s32[]{:S(2)}) async-start(s8[4718592]{0:T(1024)(128)(4,1)} %bitcast.122), calls=%async_computation.13 | async-start | bytes 8388608
  263.1 40.9 %all-to-all-start.3 = ((bf16[8,128,768]{2,1,0:T(8,128)(2,1)}), bf16[8,128,768]{2,1,0:T(8,128)(2,1)}, u32[]{:S(2)}, u32[]{:S(2)}) async-start(bf16[8,128,768]{2,1,0:T(8,128)(2,1)} %bitcast.105), calls=%async_computation.3 | async-start | bytes 3145728 | tf_op jit(solution)/shard_map/all_to_all | solution.py:147
  267.5 319.3 %all-reduce.4.cloned.1.call-start = ((), (), s32[]{:S(2)}) async-start(), calls=%async_computation.8 | async-start | bytes 18874368 | tf_op jit(solution)/shard_map/psum | solution.py:228
  324.1 10.0 %copy-start.40 = (f32[512]{0:T(512)S(1)}, f32[512]{0:T(512)}, u32[]{:S(2)}) copy-start(f32[512]{0:T(512)} %copy-done.39) | copy-start | bytes 6148
  334.1 16.7 %copy-start.3 = (f32[512,768]{1,0:T(8,128)S(1)}, f32[512,768]{1,0:T(8,128)}, u32[]{:S(2)}) copy-start(f32[512,768]{1,0:T(8,128)} %copy-done.2) | copy-start | bytes 4718596
  334.2 16.7 %copy-start.4 = (f32[512,768]{1,0:T(8,128)S(1)}, f32[512,768]{1,0:T(8,128)}, u32[]{:S(2)}) copy-start(f32[512,768]{1,0:T(8,128)} %reduce_sum.185) | copy-start | bytes 4718596
  361.9 11.1 %slice-start = ((s8[12582912]{0:T(1024)(128)(4,1)}), s8[4194304]{0:T(1024)(128)(4,1)S(1)}, s32[]{:S(2)}) async-start(s8[12582912]{0:T(1024)(128)(4,1)} %bitcast.90), calls=%async_computation.9 | async-start | bytes 8388608
  361.9 11.1 %slice-start.1 = ((s8[12582912]{0:T(1024)(128)(4,1)}), s8[4194304]{0:T(1024)(128)(4,1)S(1)}, s32[]{:S(2)}) async-start(s8[12582912]{0:T(1024)(128)(4,1)} %bitcast.90), calls=%async_computation.10 | async-start | bytes 8388608
  361.9 12.6 %slice-start.2 = ((s8[12582912]{0:T(1024)(128)(4,1)}), s8[4194304]{0:T(1024)(128)(4,1)S(1)}, s32[]{:S(2)}) async-start(s8[12582912]{0:T(1024)(128)(4,1)} %bitcast.90), calls=%async_computation.11 | async-start | bytes 8388608
  (41 other events, 166.9 us)
Sparse Core Ops, SparseCore 0:
  9.6 40.1 all-gather.2
  91.5 38.8 all-gather.4
  209.6 138.4 reduce-scatter.1
  395.4 191.3 all-reduce.3
where the time goes:
time: 612 us; the launch traced here: 601 us
  waiting for transfers between devices  194 us (32%)
  matrix products  142 us (23%)
  local copies, waits for them, and re-layouts  107 us (17%)
  other arithmetic  83.7 us (14%)
  blocking collectives  40.2 us (7%)
  starting transfers between devices  20.6 us (3%)
  between operations  14.7 us (2%)
    psum x1, waiting for transfers between devices, body(): lax.psum((gain1_grad, w_qkv_grad, w_o_grad, gain2_grad, local_counts), ('...  129 us
    psum x1, blocking collectives, body(): lax.psum((gain1_grad, w_qkv_grad, w_o_grad, gain2_grad, local_counts), ('...  40.2 us
    all_to_all x1, waiting for transfers between devices, body(): lax.all_to_all(routed_grad, 'expert', split_axis=0, concat_axis=0, tiled=...  26.3 us
    unnamed x122, local copies, waits for them, and re-layouts  23.9 us
    dot_general x2, matrix products, expert_forward(): jnp.einsum('gcf,gfd->gcd', active, down_weights, preferred_element_type=j...  20 us
    dot_general x2, matrix products, expert_backward(): jnp.einsum('gcf,gfd->gcd', hidden_grad, up_weights, preferred_element_typ...  19.5 us
    dot_general x2, matrix products, expert_forward(): jnp.einsum('gcd,gfd->gcf', rows_low, up_weights, preferred_element_type=j...  19.2 us
    reduce_sum x1, other arithmetic, body(): output = mixed_rows + jnp.sum(picked * gates[:, :, None], axis=1)  16.6 us
  transfers between devices with their start and end apart: 8, of which 5 were waited for; matrix products, arithmetic and copies ran while one was open for 48% of the time, Pallas kernels for 0%

commit v1 on v0

--- a/solution.py
+++ b/solution.py
@@ -135,7 +135,19 @@
     )
     frozen_grad_rows = grad_buffer[: FROZEN * slot_count].reshape(FROZEN, slot_count, feat_width)
     routed_grad = grad_buffer[FROZEN * slot_count :].reshape(owners, slot_count, feat_width)
-    arrived_grad = lax.all_to_all(routed_grad, "expert", split_axis=0, concat_axis=0, tiled=True)
+    ways, here = (lax.axis_size("expert"), lax.axis_index("expert"))
+    width = routed_grad.shape[0] // ways
+    shape = list(routed_grad.shape)
+    shape[0] = width
+    height = shape[0]
+    shape[0] = height * ways
+    full = jnp.zeros(shape, routed_grad.dtype)
+    for mask in range(ways):
+        part = lax.dynamic_slice_in_dim(routed_grad, (here ^ mask) * width, width, axis=0)
+        if mask:
+            part = lax.ppermute(part, "expert", [(d, d ^ mask) for d in range(ways)])
+        full = lax.dynamic_update_slice_in_dim(full, part, (here ^ mask) * height, axis=0)
+    arrived_grad = full
     flat_rows = arrived_rows.reshape(1, -1, feat_width)
     flat_grad = arrived_grad.reshape(1, -1, feat_width)
     hidden_all = jnp.einsum(

time: 612 us -> 620 us (1.013)
  local copies, waits for them, and re-layouts: 107 us -> 119 us
  waiting for transfers between devices: 194 us -> 187 us
    ppermute x0 -> x7, waiting for transfers between devices: none -> 34.4 us  [body(): part = lax.ppermute(part, 'expert', [(d, d ^ mask) for d in range(ways)])]
    all_to_all x1 -> x0, waiting for transfers between devices: 26.3 us -> none  [body(): lax.all_to_all(routed_grad, 'expert', split_axis=0, concat_axis=0, tiled=...]
    all_to_all x1, waiting for transfers between devices: 14.8 us -> 0.01 us  [body(): lax.all_to_all(routed_rows, 'expert', split_axis=0, concat_axis=0, tiled=...]
    ppermute x0 -> x7, starting transfers between devices: none -> 9.43 us  [body(): part = lax.ppermute(part, 'expert', [(d, d ^ mask) for d in range(ways)])]
    unnamed x122 -> x124, local copies, waits for them, and re-layouts: 23.9 us -> 28.8 us
  transfers between devices with their start and end apart: 8 -> 14, of which waited for: 5 -> 7; matrix products, arithmetic and copies ran while one was open for 48% -> 48% of each run, Pallas kernels for 0% -> 0%
where the time goes in v1:
time: 620 us; the launch traced here: 610 us
  waiting for transfers between devices  187 us (30%)
  matrix products  136 us (22%)
  local copies, waits for them, and re-layouts  119 us (19%)
  other arithmetic  87.7 us (14%)
  blocking collectives  40.2 us (6%)
  starting transfers between devices  25.6 us (4%)
  between operations  14.7 us (2%)
    psum x1, waiting for transfers between devices, body(): lax.psum((gain1_grad, w_qkv_grad, w_o_grad, gain2_grad, local_counts), ('...  129 us
    psum x1, blocking collectives, body(): lax.psum((gain1_grad, w_qkv_grad, w_o_grad, gain2_grad, local_counts), ('...  40.2 us
    ppermute x7, waiting for transfers between devices, body(): part = lax.ppermute(part, 'expert', [(d, d ^ mask) for d in range(ways)])  34.4 us
    unnamed x124, local copies, waits for them, and re-layouts  28.8 us
    dot_general x2, matrix products, expert_forward(): jnp.einsum('gcf,gfd->gcd', active, down_weights, preferred_element_type=j...  20 us
    dot_general x2, matrix products, expert_backward(): jnp.einsum('gcf,gfd->gcd', hidden_grad, up_weights, preferred_element_typ...  19.5 us
    reduce_sum x1, other arithmetic, body(): output = mixed_rows + jnp.sum(picked * gates[:, :, None], axis=1)  16.6 us
    dot_general x2, matrix products, expert_forward(): jnp.einsum('gcd,gfd->gcf', rows_low, up_weights, preferred_element_type=j...  16.5 us
  transfers between devices with their start and end apart: 14, of which 7 were waited for; matrix products, arithmetic and copies ran while one was open for 48% of the time, Pallas kernels for 0%

profile of v1, /device:TPU:0, one launch (start us, length us, event | category | flops | bytes accessed | tf_op | source)
XLA Modules:
  0.0 610.3 jit_solution(12483238784258250351)
XLA Ops:
  74.8 7.3 %scatter_custom_fusion = bf16[1280,768]{1,0:T(8,128)(2,1)} fusion(s32[1024]{0:T(1024)S(1)} %bitcast.116, bf16[1024,768]{1,0:T(8,128)(2,1)} %reshape.407, bf16[]{:T(256)} %constant.34.clone.1), kind=kCustom, calls=%fused_computation.98 | custom fusion | bytes 1966592 | tf_op jit(solution)/shard_map/scatter | solution.py:115
  84.7 7.3 %all-to-all-start = ((bf16[8,128,768]{2,1,0:T(8,128)(2,1)}), bf16[8,128,768]{2,1,0:T(8,128)(2,1)}, u32[]{:S(2)}, u32[]{:S(2)}) async-start(bf16[8,128,768]{2,1,0:T(8,128)(2,1)} %bitcast.96), calls=%async_computation | async-start | bytes 3145728 | tf_op jit(solution)/shard_map/all_to_all | solution.py:119
  103.1 7.8 %scatter_custom_fusion.1 = bf16[1280,768]{1,0:T(8,128)(2,1)} fusion(s32[1024]{0:T(1024)S(1)} %bitcast.117, f32[1024,768]{1,0:T(8,128)} %reshape.374, f32[1024]{0:T(1024)S(1)} %mul.298, bf16[]{:T(256)} %constant.34.clone.1), kind=kCustom, calls=%fused_computation.71 | custom fusion | flops 1572864 | bytes 5115906 | tf_op jit(solution)/shard_map/scatter | solution.py:134
  128.9 11.9 %collective-permute-done.1 = bf16[1,128,768]{2,1,0:T(8,128)(2,1)S(1)} collective-permute-done((bf16[1,128,768]{2,1,0:T(8,128)(2,1)S(1)}, bf16[1,128,768]{2,1,0:T(8,128)(2,1)S(1)}, u32[]{:S(2)}, u32[]{:S(2)}) %collective-permute-start.1) | collective-permute-done | bytes 196640 | tf_op jit(solution)/shard_map/ppermute | solution.py:148
  143.0 20.1 %collective-permute-done.3 = bf16[1,128,768]{2,1,0:T(8,128)(2,1)S(1)} collective-permute-done((bf16[1,128,768]{2,1,0:T(8,128)(2,1)S(1)}, bf16[1,128,768]{2,1,0:T(8,128)(2,1)S(1)}, u32[]{:S(2)}, u32[]{:S(2)}) %collective-permute-start.3) | collective-permute-done | bytes 196640 | tf_op jit(solution)/shard_map/ppermute | solution.py:148
  165.8 7.7 %fusion.19 = f32[1024,3072]{1,0:T(8,128)S(1)} fusion(bf16[1024,768]{1,0:T(8,128)(2,1)} %bitcast.14, bf16[1,3072,768]{2,1,0:T(8,128)(2,1)} %all-gather.3.cloned.1.call-done), kind=kOutput, calls=%fused_computation.32 | convolution fusion | flops 4831838208 | bytes 18874368 | tf_op jit(solution)/shard_map/gcd,gfd->gcf/dot_general | solution.py:19
  178.1 9.4 %fusion.98 = f32[3072,768]{0,1:T(8,128)} fusion(bf16[1024,768]{1,0:T(8,128)(2,1)} %bitcast.22, f32[1024,3072]{1,0:T(8,128)S(1)} %fusion.19), kind=kOutput, calls=%fused_computation.162 | convolution fusion | flops 4860149760 | bytes 23592960 | tf_op jit(solution)/shard_map/dot_general | solution.py:176
  187.5 15.8 %fusion.6 = bf16[1024,3072]{1,0:T(8,128)(2,1)S(1)} fusion(f32[1024,3072]{1,0:T(8,128)} %copy-done.49, bf16[1024,768]{1,0:T(8,128)(2,1)} %bitcast.22, bf16[1,3072,768]{2,1,0:T(8,128)(2,1)} %all-gather.5.cloned.1.call-done), kind=kOutput, calls=%fused_computation.13 | convolution fusion | flops 4894752768 | bytes 25165824 | tf_op jit(solution)/shard_map/gcd,gfd->gcf/dot_general | solution.py:28
  203.3 8.2 %fusion.105 = f32[3072,768]{0,1:T(8,128)S(1)} fusion(bf16[1024,3072]{1,0:T(8,128)(2,1)S(1)} %fusion.6, bf16[1024,768]{1,0:T(8,128)(2,1)} %bitcast.14), kind=kOutput, calls=%fused_computation.168 | convolution fusion | flops 4831838208 | bytes 17301504 | tf_op jit(solution)/shard_map/dot_general | solution.py:173
  211.6 7.0 %pad_maximum_fusion = f32[3072,1536]{0,1:T(8,128)} fusion(f32[3072,768]{0,1:T(8,128)S(1)} %copy-done.11, f32[3072,768]{0,1:T(8,128)S(1)} %fusion.105), kind=kLoop, calls=%fused_computation.4 | loop fusion | flops 4718592 | bytes 37748736 | tf_op jit(solution)/shard_map/concatenate | solution.py:180
  218.6 12.5 %fusion.40 = bf16[1024,768]{1,0:T(8,128)(2,1)} fusion(bf16[1,3072,768]{2,1,0:T(8,128)(2,1)} %all-gather.5.cloned.1.call-done, f32[1024,3072]{1,0:T(8,128)} %copy-done.49), kind=kOutput, calls=%fused_computation.65 | convolution fusion | flops 4860936192 | bytes 18874368 | tf_op jit(solution)/shard_map/gcf,gfd->gcd/dot_general | solution.py:21
  238.5 8.8 %fusion.104 = f32[2,128,3072]{2,1,0:T(8,128)S(1)} fusion(bf16[2,128,768]{2,1,0:T(8,128)(2,1)S(1)} %bitcast.104, bf16[2,3072,768]{2,1,0:T(8,128)(2,1)} %param.24), kind=kOutput, calls=%fused_computation.167 | convolution fusion | flops 1207959552 | bytes 12976128 | tf_op jit(solution)/shard_map/gcd,gfd->gcf/dot_general | solution.py:19
  247.4 7.5 %fusion.63 = bf16[2,128,768]{2,1,0:T(8,128)(2,1)} fusion(bf16[2,3072,768]{2,1,0:T(8,128)(2,1)} %param.25, f32[2,128,3072]{2,1,0:T(8,128)S(1)} %fusion.104), kind=kOutput, calls=%fused_computation.91 | convolution fusion | flops 1215234048 | bytes 12976128 | tf_op jit(solution)/shard_map/gcf,gfd->gcd/dot_general | solution.py:21
  261.0 10.9 %all-to-all-done.1 = bf16[8,128,768]{2,1,0:T(8,128)(2,1)} async-done(((bf16[8,128,768]{2,1,0:T(8,128)(2,1)}), bf16[8,128,768]{2,1,0:T(8,128)(2,1)}, u32[]{:S(2)}, u32[]{:S(2)}) %all-to-all-start.1) | async-done | bytes 1572896 | tf_op jit(solution)/shard_map/all_to_all | solution.py:125
  277.7 13.3 %fusion.60 = bf16[2,128,768]{2,1,0:T(8,128)(2,1)} fusion(bf16[2,3072,768]{2,1,0:T(8,128)(2,1)} %param.24, f32[2,128,3072]{2,1,0:T(8,128)} %copy-done.19, bf16[2,128,768]{2,1,0:T(8,128)(2,1)} %bitcast.111, bf16[2,3072,768]{2,1,0:T(8,128)(2,1)} %param.25), kind=kOutput, calls=%fused_computation.90 | convolution fusion | flops 2431844352 | bytes 22806528 | tf_op jit(solution)/shard_map/gcf,gfd->gcd/dot_general | solution.py:33
  293.9 7.6 %gather_fusion = bf16[1024,768]{1,0:T(8,128)(2,1)} fusion(bf16[1280,768]{1,0:T(8,128)(2,1)} %pad_maximum_fusion.2, s32[1024]{0:T(1024)S(1)} %broadcast_clamp_fusion), kind=kCustom, calls=%fused_computation | custom fusion | bytes 3149824 | tf_op jit(solution)/shard_map/gather | solution.py:129
  301.6 11.3 %all-to-all-done.2 = bf16[8,128,768]{2,1,0:T(8,128)(2,1)} async-done(((bf16[8,128,768]{2,1,0:T(8,128)(2,1)}), bf16[8,128,768]{2,1,0:T(8,128)(2,1)}, u32[]{:S(2)}, u32[]{:S(2)}) %all-to-all-start.2) | async-done | bytes 1572896 | tf_op jit(solution)/shard_map/all_to_all | solution.py:159
  315.8 7.4 %gather_fusion.1 = bf16[1024,768]{1,0:T(8,128)(2,1)} fusion(bf16[1280,768]{1,0:T(8,128)(2,1)} %pad_maximum_fusion.3, s32[1024]{0:T(1024)S(1)} %broadcast_clamp_fusion), kind=kCustom, calls=%fused_computation.1 | custom fusion | bytes 3149824 | tf_op jit(solution)/shard_map/gather | solution.py:188
  333.0 6.8 %reduce_sum.185 = f32[512,768]{1,0:T(8,128)} reduce(f32[512,2,768]{2,1,0:T(2,128)} %reshape.386, f32[]{:T(128)} %constant.27.clone.1), dimensions={1}, to_apply=%region_14.15 | reduce | flops 393216 | bytes 4718596 | tf_op jit(solution)/shard_map/reduce_sum | solution.py:187
  343.0 16.6 %multiply_reduce_fusion.1 = f32[512,768]{1,0:T(8,128)S(1)} fusion(f32[512,2,768]{2,1,0:T(2,128)S(1)} %copy-done.6, f32[512,2]{1,0:T(8,128)} %copy.66), kind=kLoop, calls=%fused_computation.46 | loop fusion | flops 1179648 | bytes 4722688 | tf_op jit(solution)/shard_map/reduce_sum | solution.py:130
  370.8 11.0 %multiply_reduce_fusion = (f32[12,512]{1,0:T(8,128)S(1)}, f32[12,512,512]{1,2,0:T(8,128)}) fusion(f32[12,512]{1,0:T(8,128)S(1)} %copy-done.25, f32[12,512,512]{1,2,0:T(8,128)} %copy-done.1, pred[512,512]{0,1:T(8,128)(4,1)S(1)} %copy-done.15, bf16[512,12,64]{0,2,1:T(8,128)(2,1)S(1)} %bitcast.100, bf16[512,12,64]{0,2,1:T(8,128)(2,1)S(1)} %bitcast.99), kind=kOutput, calls=%fused_computation.15 | convolution fusion | flops 418375680 | bytes 27049984 | tf_op jit(solution)/shard_map/qhd,khd->hqk/dot_general | solution.py:207
  383.4 7.0 %multiply_convert_fusion = bf16[12,512,512]{1,2,0:T(8,128)(2,1)S(1)} fusion(f32[12,512,512]{1,2,0:T(8,128)} %get-tuple-element.68, f32[12,512]{1,0:T(8,128)S(1)} %get-tuple-element.67, f32[12,512]{1,0:T(8,128)S(1)} %copy-done.25, f32[12,512,512]{1,2,0:T(8,128)S(1)} %bitcast.91, pred[512,512]{0,1:T(8,128)(4,1)S(1)} %copy-done.15), kind=kLoop, calls=%fused_computation.14 | loop fusion | flops 18874368 | bytes 31768576 | tf_op jit(solution)/shard_map/convert_element_type | solution.py:211
  410.9 40.2 %all-reduce = (f32[768]{0:T(1024)}, f32[768]{0:T(1024)}, f32[10]{0:T(128)}) all-reduce(f32[768]{0:T(1024)} %get-tuple-element.38, f32[768]{0:T(1024)} %get-tuple-element.36, f32[10]{0:T(128)} %convert_element_type.136), channel_id=1, replica_groups=mesh['dp'=4,'expert'=8] {'dp','expert'}, use_global_device_ids=true, to_apply=%region_21.22 | all-reduce | flops 1546 | bytes 12368 | tf_op jit(solution)/shard_map/psum | solution.py:240
  466.8 128.8 %all-reduce.4.cloned.1.call-done = (f32[768,2304]{1,0:T(8,128)}, f32[768,768]{1,0:T(8,128)}) async-done(((f32[768,2304]{1,0:T(8,128)}, f32[768,768]{1,0:T(8,128)}), (f32[768,2304]{1,0:T(8,128)}, f32[768,768]{1,0:T(8,128)})) %all-reduce.4.cloned.1.call-update) | async-done | bytes 9437200 | tf_op jit(solution)/shard_map/psum | solution.py:240
  (233 shorter events, 203.3 us)
Async XLA Ops:
  7.2 24.4 %copy-start = (bf16[768,2304]{1,0:T(8,128)(2,1)S(1)}, bf16[768,2304]{1,0:T(8,128)(2,1)}, u32[]{:S(2)}) copy-start(bf16[768,2304]{1,0:T(8,128)(2,1)} %param.21) | copy-start | bytes 10616836
  7.2 158.6 %all-gather.3.cloned.1.call-start = ((), (), s32[]{:S(2)}) async-start(), calls=%async_computation.4 | async-start | bytes 5898240 | tf_op jit(solution)/shard_map/all_gather | solution.py:70
  7.9 179.5 %all-gather.5.cloned.1.call-start = ((), (), s32[]{:S(2)}) async-start(), calls=%async_computation.5 | async-start | bytes 5898240 | tf_op jit(solution)/shard_map/all_gather | solution.py:71
  14.9 19.9 %copy-start.31 = (f32[512]{0:T(512)}, f32[512]{0:T(512)S(1)}, u32[]{:S(2)}) copy-start(f32[512]{0:T(512)S(1)} %broadcast_multiply_fusion.2) | copy-start | bytes 6148
  16.4 11.6 %copy-start.36 = (f32[512]{0:T(512)}, f32[512]{0:T(512)S(1)}, u32[]{:S(2)}) copy-start(f32[512]{0:T(512)S(1)} %fusion.45) | copy-start | bytes 6148
  59.8 13.5 %copy-start.33 = (f32[512]{0:T(512)}, f32[512]{0:T(512)S(1)}, u32[]{:S(2)}) copy-start(f32[512]{0:T(512)S(1)} %fusion.78) | copy-start | bytes 6148
  84.7 81.1 %all-to-all-start = ((bf16[8,128,768]{2,1,0:T(8,128)(2,1)}), bf16[8,128,768]{2,1,0:T(8,128)(2,1)}, u32[]{:S(2)}, u32[]{:S(2)}) async-start(bf16[8,128,768]{2,1,0:T(8,128)(2,1)} %bitcast.96), calls=%async_computation | async-start | bytes 3145728 | tf_op jit(solution)/shard_map/all_to_all | solution.py:119
  92.0 363.8 %reduce-scatter.2.cloned.1.call-start = ((), (), s32[]{:S(2)}) async-start(), calls=%async_computation.6 | async-start | bytes 23592960 | tf_op jit(solution)/shard_map/reduce_scatter | solution.py:179
  117.1 10.3 %collective-permute-start = (bf16[1,128,768]{2,1,0:T(8,128)(2,1)S(1)}, bf16[1,128,768]{2,1,0:T(8,128)(2,1)S(1)}, u32[]{:S(2)}, u32[]{:S(2)}) collective-permute-start(bf16[1,128,768]{2,1,0:T(8,128)(2,1)S(1)} %get-tuple-element.61), channel_id=1, source_target_pairs={{0,1},{1,0},{2,3},{3,2},{4,5},{5,4},{6,7},{7,6},{8,9},{9,8},{10,11... | collective-permute-start | bytes 589832 | tf_op jit(solution)/shard_map/ppermute | solution.py:148
  119.1 21.7 %collective-permute-start.1 = (bf16[1,128,768]{2,1,0:T(8,128)(2,1)S(1)}, bf16[1,128,768]{2,1,0:T(8,128)(2,1)S(1)}, u32[]{:S(2)}, u32[]{:S(2)}) collective-permute-start(bf16[1,128,768]{2,1,0:T(8,128)(2,1)S(1)} %get-tuple-element.60), channel_id=1, source_target_pairs={{0,2},{1,3},{2,0},{3,1},{4,6},{5,7},{6,4},{7,5},{8,10},{9,11},{10,... | collective-permute-start | bytes 589832 | tf_op jit(solution)/shard_map/ppermute | solution.py:148
  120.5 44.6 %collective-permute-start.6 = (bf16[1,128,768]{2,1,0:T(8,128)(2,1)S(1)}, bf16[1,128,768]{2,1,0:T(8,128)(2,1)S(1)}, u32[]{:S(2)}, u32[]{:S(2)}) collective-permute-start(bf16[1,128,768]{2,1,0:T(8,128)(2,1)S(1)} %get-tuple-element.55), channel_id=1, source_target_pairs={{0,7},{1,6},{2,5},{3,4},{4,3},{5,2},{6,1},{7,0},{8,15},{9,14},{10,... | collective-permute-start | bytes 589832 | tf_op jit(solution)/shard_map/ppermute | solution.py:148
  122.9 41.5 %collective-permute-start.5 = (bf16[1,128,768]{2,1,0:T(8,128)(2,1)S(1)}, bf16[1,128,768]{2,1,0:T(8,128)(2,1)S(1)}, u32[]{:S(2)}, u32[]{:S(2)}) collective-permute-start(bf16[1,128,768]{2,1,0:T(8,128)(2,1)S(1)} %get-tuple-element.56), channel_id=1, source_target_pairs={{0,6},{1,7},{2,4},{3,5},{4,2},{5,3},{6,0},{7,1},{8,14},{9,15},{10,... | collective-permute-start | bytes 589832 | tf_op jit(solution)/shard_map/ppermute | solution.py:148
  124.4 39.4 %collective-permute-start.4 = (bf16[1,128,768]{2,1,0:T(8,128)(2,1)S(1)}, bf16[1,128,768]{2,1,0:T(8,128)(2,1)S(1)}, u32[]{:S(2)}, u32[]{:S(2)}) collective-permute-start(bf16[1,128,768]{2,1,0:T(8,128)(2,1)S(1)} %get-tuple-element.57), channel_id=1, source_target_pairs={{0,5},{1,4},{2,7},{3,6},{4,1},{5,0},{6,3},{7,2},{8,13},{9,12},{10,... | collective-permute-start | bytes 589832 | tf_op jit(solution)/shard_map/ppermute | solution.py:148
  127.4 14.8 %collective-permute-start.2 = (bf16[1,128,768]{2,1,0:T(8,128)(2,1)S(1)}, bf16[1,128,768]{2,1,0:T(8,128)(2,1)S(1)}, u32[]{:S(2)}, u32[]{:S(2)}) collective-permute-start(bf16[1,128,768]{2,1,0:T(8,128)(2,1)S(1)} %get-tuple-element.59), channel_id=1, source_target_pairs={{0,3},{1,2},{2,1},{3,0},{4,7},{5,6},{6,5},{7,4},{8,11},{9,10},{10,... | collective-permute-start | bytes 589832 | tf_op jit(solution)/shard_map/ppermute | solution.py:148
  140.8 22.3 %collective-permute-start.3 = (bf16[1,128,768]{2,1,0:T(8,128)(2,1)S(1)}, bf16[1,128,768]{2,1,0:T(8,128)(2,1)S(1)}, u32[]{:S(2)}, u32[]{:S(2)}) collective-permute-start(bf16[1,128,768]{2,1,0:T(8,128)(2,1)S(1)} %get-tuple-element.58), channel_id=1, source_target_pairs={{0,4},{1,5},{2,6},{3,7},{4,0},{5,1},{6,2},{7,3},{8,12},{9,13},{10,... | collective-permute-start | bytes 589832 | tf_op jit(solution)/shard_map/ppermute | solution.py:148
  231.1 40.9 %all-to-all-start.1 = ((bf16[8,128,768]{2,1,0:T(8,128)(2,1)}), bf16[8,128,768]{2,1,0:T(8,128)(2,1)}, u32[]{:S(2)}, u32[]{:S(2)}) async-start(bf16[8,128,768]{2,1,0:T(8,128)(2,1)} %bitcast.106), calls=%async_computation.1 | async-start | bytes 3145728 | tf_op jit(solution)/shard_map/all_to_all | solution.py:125
  238.5 16.3 %slice-start.3 = ((s8[4718592]{0:T(1024)(128)(4,1)}), s8[524288]{0:T(1024)(128)(4,1)S(1)}, s32[]{:S(2)}) async-start(s8[4718592]{0:T(1024)(128)(4,1)} %bitcast.122), calls=%async_computation.11 | async-start | bytes 1048576
  238.5 16.3 %slice-start.5 = ((s8[6291456]{0:T(1024)(128)(4,1)}), s8[4194304]{0:T(1024)(128)(4,1)S(1)}, s32[]{:S(2)}) async-start(s8[6291456]{0:T(1024)(128)(4,1)} %bitcast.127), calls=%async_computation.13 | async-start | bytes 8388608
  272.0 40.9 %all-to-all-start.2 = ((bf16[8,128,768]{2,1,0:T(8,128)(2,1)}), bf16[8,128,768]{2,1,0:T(8,128)(2,1)}, u32[]{:S(2)}, u32[]{:S(2)}) async-start(bf16[8,128,768]{2,1,0:T(8,128)(2,1)} %bitcast.105), calls=%async_computation.2 | async-start | bytes 3145728 | tf_op jit(solution)/shard_map/all_to_all | solution.py:159
  276.3 319.3 %all-reduce.4.cloned.1.call-start = ((), (), s32[]{:S(2)}) async-start(), calls=%async_computation.7 | async-start | bytes 18874368 | tf_op jit(solution)/shard_map/psum | solution.py:240
  343.0 16.7 %copy-start.3 = (f32[512,768]{1,0:T(8,128)S(1)}, f32[512,768]{1,0:T(8,128)}, u32[]{:S(2)}) copy-start(f32[512,768]{1,0:T(8,128)} %copy-done.2) | copy-start | bytes 4718596
  343.0 16.7 %copy-start.4 = (f32[512,768]{1,0:T(8,128)S(1)}, f32[512,768]{1,0:T(8,128)}, u32[]{:S(2)}) copy-start(f32[512,768]{1,0:T(8,128)} %reduce_sum.185) | copy-start | bytes 4718596
  370.7 11.1 %slice-start = ((s8[12582912]{0:T(1024)(128)(4,1)}), s8[4194304]{0:T(1024)(128)(4,1)S(1)}, s32[]{:S(2)}) async-start(s8[12582912]{0:T(1024)(128)(4,1)} %bitcast.90), calls=%async_computation.8 | async-start | bytes 8388608
  370.8 12.6 %slice-start.2 = ((s8[12582912]{0:T(1024)(128)(4,1)}), s8[4194304]{0:T(1024)(128)(4,1)S(1)}, s32[]{:S(2)}) async-start(s8[12582912]{0:T(1024)(128)(4,1)} %bitcast.90), calls=%async_computation.10 | async-start | bytes 8388608
  (48 other events, 248.8 us)
Sparse Core Ops, SparseCore 0:
  9.6 40.1 all-gather.2
  51.3 37.4 all-gather.4
  218.7 138.2 reduce-scatter.1
  404.2 191.3 all-reduce.3
